TPU v7x, 32 devices: a whole 2x2x4 slice. The times are simulated.
32 devices in a mesh: dp: 4 (over y, core), seq: 8 (over z, x).
Axes of the slice: x: 2, y: 2, z: 4, core: 2. Of those that a mesh axis runs over, the one named last changes fastest.
Arguments:
- tokens: bfloat16 [4, 24, 256, 1280], P('dp', 'seq'), may hold values from -6 to 6
- clip_ids: int32 [4, 24], P('dp'), may hold values from 0 to 5, never falling along the last dimension, each value on 1 to 12 neighbouring positions
- ln_gain: float32 [1280], replicated, may hold values from 0.1 to 1.9
- w_qkv: bfloat16 [1280, 1920], P(None, 'dp'), may hold values from -0.15625 to 0.15625
- w_out: bfloat16 [640, 1280], P(None, 'dp'), may hold values from -0.25 to 0.25
Outputs:
- output: bfloat16 [4, 24, 256, 1280], P('dp', 'seq')
Inputs may be any that keep to these rules, and one draw needn't show every extreme that they name: `clip_ids`: in each batch the clip numbers never fall along the frames, every clip number occurs, each clip covers 1 to 12 consecutive frames, and some clip covers exactly 12.
All inputs are finite; a program needn't handle non-finite values.
Results may differ from a plain program's by a relative error of at most 0.006.
Values may be sent and summed in bfloat16 or wider, within the bound.
A program may use at most 64 MiB of HBM per device.

v0:
```python
import math

import jax
import jax.numpy as jnp
from jax import lax
from jax.sharding import PartitionSpec as P

HS = 80
HEADS = 8
HD = 640


norm_eps = 1e-05


def layer_norm(block, ln_gain):
    values = block.astype(jnp.float32)
    center = jnp.mean(values, axis=-1, keepdims=True)
    spread = jnp.mean(jnp.square(values - center), axis=-1, keepdims=True)
    return ((values - center) * lax.rsqrt(spread + norm_eps) * ln_gain).astype(jnp.bfloat16)


def split_heads(projected):
    queries = (projected[:, :HD] * (1.0 / math.sqrt(HS))).astype(jnp.bfloat16)
    keys = projected[:, HD : 2 * HD].astype(jnp.bfloat16)
    values = projected[:, 2 * HD :].astype(jnp.bfloat16)
    return (queries, keys, values)


def attend(queries, keys, values, clip_row):
    scores = jnp.einsum("flhe,glhe->lhfg", queries, keys, preferred_element_type=jnp.float32)
    same_clip = clip_row[:, None] == clip_row[None, :]
    raised = jnp.where(same_clip, jnp.exp(scores), jnp.zeros_like(scores))
    attn_probs = (raised / jnp.sum(raised, axis=-1, keepdims=True)).astype(jnp.bfloat16)
    return jnp.einsum(
        "lhfg,glhe->flhe", attn_probs, values, preferred_element_type=jnp.float32
    ).astype(jnp.bfloat16)


def shards(tokens, clip_ids, ln_gain, w_qkv, w_out):
    width = tokens.shape[3]
    clip_row = clip_ids[0]
    frames = clip_row.shape[0]
    local_frames = tokens.shape[1]
    patches = tokens.shape[2]
    moved = lax.all_to_all(tokens, "seq", split_axis=2, concat_axis=1, tiled=True)
    places = moved.shape[2]
    normed = layer_norm(moved, ln_gain).reshape(frames * places, width)

    def column_block(piece, start):
        return jnp.dot(normed, piece, preferred_element_type=jnp.float32)

    queries, keys, values = split_heads(
        column_block(lax.all_gather(w_qkv, "dp", axis=1, tiled=True), jnp.int32(0))
    )
    head_shape = (frames, places, HEADS, HS)
    mixed = attend(
        queries.reshape(head_shape), keys.reshape(head_shape), values.reshape(head_shape), clip_row
    )
    mixed = lax.all_to_all(
        mixed.reshape(1, frames, places, HD), "seq", split_axis=1, concat_axis=2, tiled=True
    )
    row_count = local_frames * patches
    rows_in = mixed.reshape(row_count, HD)

    def column_block(piece, start):
        return jnp.dot(rows_in, piece, preferred_element_type=jnp.float32)

    update = column_block(lax.all_gather(w_out, "dp", axis=1, tiled=True), jnp.int32(0))
    summed = tokens.reshape(row_count, width).astype(jnp.float32) + update
    return summed.astype(jnp.bfloat16).reshape(tokens.shape)


def solution(mesh):
    placed = (P("dp", "seq", None, None), P("dp", None), P(), P(None, "dp"), P(None, "dp"))
    return jax.shard_map(
        shards, mesh=mesh, in_specs=placed, out_specs=P("dp", "seq", None, None), check_vma=False
    )
```

profile of v0, /device:TPU:0, one launch (start us, length us, event | category | flops | bytes accessed | tf_op | source)
XLA Modules:
  0.0 151.9 jit_solution(18149255715372341711)
XLA Ops:
  6.5 0.0 all-gather.3.cloned.1.call-start
  6.5 0.7 all-gather.3.cloned.1.call-update
  7.3 4.8 %copy.35 = bf16[1,3,256,1280]{3,1,0,2:T(4,128)(2,1)} copy(bf16[1,3,256,1280]{3,2,1,0:T(8,128)(2,1)} %param.5) | data formatting | bytes 3932160 | tf_op args[0]
  12.0 0.0 copy-start.2
  12.0 7.4 %all-to-all-start = ((bf16[1,3,256,1280]{3,1,0,2:T(4,128)(2,1)}), bf16[1,3,256,1280]{3,1,0,2:T(4,128)(2,1)S(1)}, u32[]{:S(2)}, u32[]{:S(2)}) async-start(bf16[1,3,256,1280]{3,1,0,2:T(4,128)(2,1)} %copy.35), calls=%async_computation | async-start | bytes 5242880 | tf_op jit(solution)/shard_map/all_to_all | solution.py:46
  19.4 0.0 all-gather.5.cloned.1.call-start
  19.5 0.7 all-gather.5.cloned.1.call-update
  20.2 0.0 copy-done.2
  20.2 0.1 broadcast_compare_fusion
  20.3 58.6 %all-to-all-done = bf16[1,3,256,1280]{3,1,0,2:T(4,128)(2,1)S(1)} async-done(((bf16[1,3,256,1280]{3,1,0,2:T(4,128)(2,1)}), bf16[1,3,256,1280]{3,1,0,2:T(4,128)(2,1)S(1)}, u32[]{:S(2)}, u32[]{:S(2)}) %all-to-all-start) | async-done | bytes 1966112 | tf_op jit(solution)/shard_map/all_to_all | solution.py:46
  78.9 2.3 %convert_bitcast_fusion = (f32[1,8,3,32,1280]{4,3,1,2,0:T(8,128)}, bf16[1,3,256,1280]{3,2,1,0:T(8,128)(2,1)S(1)}) fusion(bf16[1,3,256,1280]{3,1,0,2:T(4,128)(2,1)S(1)} %all-to-all-done), kind=kLoop, calls=%fused_computation.1 | loop fusion | flops 983040 | bytes 7864320 | tf_op jit(solution)/shard_map/convert_element_type | solution.py:17
  81.2 0.3 fusion.5
  81.6 0.7 multiply_reduce_fusion
  82.3 0.1 rsqrt.12
  82.4 0.1 div.17
  82.4 0.0 copy-start.1
  82.4 2.4 %copy.37 = f32[1,8,3,32,1280]{4,3,2,1,0:T(8,128)S(1)} copy(f32[1,8,3,32,1280]{4,3,1,2,0:T(8,128)} %get-tuple-element.5) | data formatting | bytes 7864320 | tf_op jit(solution)/shard_map/convert_element_type | solution.py:17
  84.9 0.0 copy-done.1
  84.9 0.6 fusion.2
  85.4 0.0 all-gather.3.cloned.1.call-done
  85.5 8.5 %fusion.18 = (bf16[768,1920]{1,0:T(8,128)(2,1)S(1)}, f32[768,1920]{1,0:T(8,128)}) fusion(bf16[768,1280]{1,0:T(8,128)(2,1)S(1)} %fusion.2, bf16[1280,1920]{0,1:T(8,128)(2,1)} %all-gather.3.cloned.1.call-done), kind=kOutput, calls=%fused_computation.27 | convolution fusion | flops 3776348160 | bytes 15728640 | tf_op jit(solution)/shard_map/dot_general | solution.py:51
  94.0 0.2 fusion.17
  94.2 1.6 %reshape.90 = bf16[24,32,8,80]{3,2,1,0:T(8,128)(2,1)S(1)} reshape(bf16[768,640]{1,0:T(8,128)(2,1)S(1)} %get-tuple-element.8) | data formatting | bytes 1966080 | tf_op jit(solution)/shard_map/reshape | solution.py:58
  95.8 1.7 %fusion.6 = bf16[768,640]{1,0:T(8,128)(2,1)S(1)} fusion(f32[768,1920]{1,0:T(8,128)} %get-tuple-element.10), kind=kLoop, calls=%fused_computation.13 | loop fusion | flops 983040 | bytes 2949120 | tf_op jit(solution)/shard_map/convert_element_type | solution.py:24
  97.5 2.5 %reshape.89 = bf16[24,32,8,80]{3,2,1,0:T(8,128)(2,1)} reshape(bf16[768,640]{1,0:T(8,128)(2,1)S(1)} %fusion.6) | data formatting | bytes 1966080 | tf_op jit(solution)/shard_map/reshape | solution.py:58
  100.0 5.7 %fusion.4 = (f32[32,8,24]{2,1,0:T(8,128)S(1)}, f32[32,8,24,24]{2,3,1,0:T(8,128)}) fusion(pred[24,24]{0,1:T(8,128)(4,1)S(1)} %broadcast_compare_fusion, bf16[24,32,8,80]{3,2,1,0:T(8,128)(2,1)S(1)} %reshape.90, bf16[24,32,8,80]{3,2,1,0:T(8,128)(2,1)} %reshape.89), kind=kOutput, calls=%fused_computation.10 | convolution fusion | flops 23881728 | bytes 2581056 | tf_op jit(solution)/shard_map/flhe,glhe->lhfg/dot_general | solution.py:31
  105.7 1.6 %reshape.88 = bf16[24,32,8,80]{3,2,1,0:T(8,128)(2,1)S(1)} reshape(bf16[768,640]{1,0:T(8,128)(2,1)S(1)} %get-tuple-element.7) | data formatting | bytes 1966080 | tf_op jit(solution)/shard_map/reshape | solution.py:58
  107.3 3.4 %fusion.13 = bf16[24,32,8,80]{3,0,2,1:T(8,128)(2,1)S(1)} fusion(f32[32,8,24,24]{2,3,1,0:T(8,128)} %get-tuple-element.12, f32[32,8,24]{2,1,0:T(8,128)S(1)} %get-tuple-element.11, pred[24,24]{0,1:T(8,128)(4,1)S(1)} %broadcast_compare_fusion, bf16[24,32,8,80]{3,2,1,0:T(8,128)(2,1)S(1)} %reshape.88), kind=kOutput, calls=%fused_computation.21 | convolution fusion | flops 24526848 | bytes 2581056 | tf_op jit(solution)/shard_map/lhfg,glhe->flhe/dot_general | solution.py:35
  110.7 0.3 copy.44
  111.1 1.2 reshape.91
  112.3 0.0 copy-start
  112.3 28.2 %all_to_all.24 = bf16[1,24,32,640]{3,2,0,1:T(8,128)(2,1)S(1)} all-to-all(bf16[1,24,32,640]{3,2,0,1:T(8,128)(2,1)S(1)} %bitcast.36), channel_id=1, replica_groups=mesh['dp'=4,'seq'=8] {'seq'}, dimensions={1} | all-to-all | bytes 1966080 | tf_op jit(solution)/shard_map/all_to_all | solution.py:60
  140.5 0.1 copy.46
  140.6 0.0 all-gather.5.cloned.1.call-done
  140.6 0.0 copy-done
  140.6 4.4 %fusion.3 = bf16[768,1280]{1,0:T(8,128)(2,1)} fusion(bf16[768,640]{1,0:T(8,128)(2,1)S(1)} %bitcast.39, bf16[640,1280]{0,1:T(8,128)(2,1)} %all-gather.5.cloned.1.call-done, bf16[768,1280]{1,0:T(8,128)(2,1)S(1)} %bitcast.38), kind=kOutput, calls=%fused_computation.7 | convolution fusion | flops 1261240320 | bytes 6553600 | tf_op jit(solution)/shard_map/dot_general | solution.py:67
  (4 shorter events, 0.0 us)
Async XLA Ops:
  6.5 78.9 %all-gather.3.cloned.1.call-start = ((), (), s32[]{:S(2)}) async-start(), calls=%async_computation.2 | async-start | bytes 6144000 | tf_op jit(solution)/shard_map/all_gather | solution.py:54
  12.0 8.2 %copy-start.2 = (s32[1,24]{1,0:T(1,128)S(1)}, s32[1,24]{1,0:T(1,128)}, u32[]{:S(2)}) copy-start(s32[1,24]{1,0:T(1,128)} %param.6) | copy-start | bytes 292
  12.0 66.9 %all-to-all-start = ((bf16[1,3,256,1280]{3,1,0,2:T(4,128)(2,1)}), bf16[1,3,256,1280]{3,1,0,2:T(4,128)(2,1)S(1)}, u32[]{:S(2)}, u32[]{:S(2)}) async-start(bf16[1,3,256,1280]{3,1,0,2:T(4,128)(2,1)} %copy.35), calls=%async_computation | async-start | bytes 5242880 | tf_op jit(solution)/shard_map/all_to_all | solution.py:46
  19.4 121.2 %all-gather.5.cloned.1.call-start = ((), (), s32[]{:S(2)}) async-start(), calls=%async_computation.3 | async-start | bytes 2048000 | tf_op jit(solution)/shard_map/all_gather | solution.py:69
  82.4 2.4 %copy-start.1 = (f32[1280]{0:T(1024)S(1)}, f32[1280]{0:T(1024)}, u32[]{:S(2)}) copy-start(f32[1280]{0:T(1024)} %param.7) | copy-start | bytes 15364
  112.3 28.3 %copy-start = (bf16[1,3,256,1280]{3,2,1,0:T(8,128)(2,1)S(1)}, bf16[1,3,256,1280]{3,2,1,0:T(8,128)(2,1)}, u32[]{:S(2)}) copy-start(bf16[1,3,256,1280]{3,2,1,0:T(8,128)(2,1)} %param.5) | copy-start | bytes 5898244
Sparse Core Ops, SparseCore 0:
  8.9 41.2 all-gather.2
  51.8 19.9 all-gather.4
where the time goes:
time: 152 us
  waiting for transfers between devices  60.1 us (40%)
  blocking collectives  28.2 us (19%)
  matrix products  22 us (14%)
  local copies, waits for them, and re-layouts  14.9 us (10%)
  between operations  13.6 us (9%)
  starting transfers between devices  7.45 us (5%)
  other arithmetic  5.69 us (4%)
    all_to_all x1, waiting for transfers between devices, shards(): lax.all_to_all(tokens, 'seq', split_axis=2, concat_axis=1, tiled=True)  58.6 us
    all_to_all x1, blocking collectives, shards(): lax.all_to_all(mixed.reshape(1, frames, places, HD), 'seq', split_axis=1,...  28.2 us
    dot_general x1, matrix products, column_block(): return jnp.dot(normed, piece, preferred_element_type=jnp.float32)  8.52 us
    all_to_all x1, starting transfers between devices, shards(): lax.all_to_all(tokens, 'seq', split_axis=2, concat_axis=1, tiled=True)  7.41 us
    dot_general x1, matrix products, attend(): jnp.einsum('flhe,glhe->lhfg', queries, keys, preferred_element_type=jnp.f...  5.69 us
    unnamed x7, local copies, waits for them, and re-layouts  4.77 us
    dot_general x1, matrix products, column_block(): return jnp.dot(rows_in, piece, preferred_element_type=jnp.float32)  4.43 us
    dot_general x1, matrix products, attend(): jnp.einsum('lhfg,glhe->flhe', attn_probs, values, preferred_element_type=...  3.4 us
  transfers between devices with their start and end apart: 3, of which 1 were waited for; matrix products, arithmetic and copies ran while one was open for 25% of the time, Pallas kernels for 0%

commit v1 on v0

v1 whole, which is shorter than its diff:
```python
import functools
import math

import jax
import jax.numpy as jnp
from jax import lax
from jax.experimental import pallas as pl
from jax.experimental.pallas import tpu as pltpu
from jax.sharding import PartitionSpec as P

HS = 80
HEADS = 8
HD = 640
LANES = 128
SUB = 8

norm_eps = 1e-05
MESH = pl.DeviceIdType.MESH
F32, BF16 = jnp.float32, jnp.bfloat16


def kernel(n, ndp, chunks, ch, nb, tokens, w_qkv, w_out, gain, bias, out,
           recv, mix_out, mix_in, wq_st, wq, wo_st, wo, q_s, k_s, v_s, o_s, tok,
           t_send, t_recv, m_send, m_recv, w_send, w_recv, f_send, f_recv, loc):
    me = lax.axis_index("seq")
    dp = lax.axis_index("dp")
    lf, width = tokens.shape[1], tokens.shape[3]
    lp = chunks * ch
    frames = n * lf
    half = ndp // 2
    partner = dp + 1 - 2 * lax.rem(dp, 2)
    groups = ch // SUB

    def peer(k):
        return lax.rem(me + k, n)

    def far(j):
        return lax.rem(dp + 2 * j, ndp)

    barrier = pltpu.get_barrier_semaphore()
    for k in range(1, n):
        pl.semaphore_signal(barrier, inc=1, device_id=(dp, peer(k)), device_id_type=MESH)
    for j in range(1, half):
        pl.semaphore_signal(barrier, inc=1, device_id=(far(j), me), device_id_type=MESH)
    pl.semaphore_signal(barrier, inc=1, device_id=(partner, me), device_id_type=MESH)
    pl.semaphore_wait(barrier, n - 1 + half)

    shards = ((w_qkv, wq_st), (w_out, wo_st))

    def w_copy(which, j):
        source, stage = shards[which]
        target = far(j) if j else partner
        return pltpu.make_async_remote_copy(
            src_ref=source, dst_ref=stage.at[dp],
            send_sem=w_send.at[which, j], recv_sem=w_recv.at[which, j],
            device_id=(target, me), device_id_type=MESH)

    def w_arrived(which, j):
        source, stage = shards[which]
        origin = lax.rem(dp - 2 * j + ndp, ndp) if j else partner
        return pltpu.make_async_remote_copy(
            src_ref=source, dst_ref=stage.at[origin],
            send_sem=w_send.at[which, j], recv_sem=w_recv.at[which, j],
            device_id=(partner, me), device_id_type=MESH)

    def forward(which, j):
        stage = shards[which][1]
        origin = lax.rem(dp - 2 * j + ndp, ndp)
        return pltpu.make_async_remote_copy(
            src_ref=stage.at[origin], dst_ref=stage.at[origin],
            send_sem=f_send.at[which, j], recv_sem=f_recv.at[which, j],
            device_id=(partner, me), device_id_type=MESH)

    def forwarded(which, j):
        stage = shards[which][1]
        origin = lax.rem(partner - 2 * j + ndp, ndp)
        return pltpu.make_async_remote_copy(
            src_ref=stage.at[origin], dst_ref=stage.at[origin],
            send_sem=f_send.at[which, j], recv_sem=f_recv.at[which, j],
            device_id=(partner, me), device_id_type=MESH)

    def rows_of(owner, c):
        return pl.ds(pl.multiple_of(owner * lp + c * ch, SUB), ch)

    def t_copy(c, k):
        return pltpu.make_async_remote_copy(
            src_ref=tokens.at[0, :, rows_of(peer(k), c), :],
            dst_ref=recv.at[c, pl.ds(me * lf, lf)],
            send_sem=t_send.at[c, k], recv_sem=t_recv.at[c, k],
            device_id=(dp, peer(k)), device_id_type=MESH)

    def t_arrived(c, k):
        origin = lax.rem(me - k + n, n)
        return pltpu.make_async_remote_copy(
            src_ref=tokens.at[0, :, rows_of(origin, c), :],
            dst_ref=recv.at[c, pl.ds(origin * lf, lf)],
            send_sem=t_send.at[c, k], recv_sem=t_recv.at[c, k],
            device_id=(dp, origin), device_id_type=MESH)

    def t_own(c):
        return pltpu.make_async_copy(
            tokens.at[0, :, rows_of(me, c), :], recv.at[c, pl.ds(me * lf, lf)], t_recv.at[c, 0])

    def m_copy(c, k):
        return pltpu.make_async_remote_copy(
            src_ref=mix_out.at[c, pl.ds(peer(k) * lf, lf)],
            dst_ref=mix_in.at[c, me],
            send_sem=m_send.at[c, k], recv_sem=m_recv.at[c, k],
            device_id=(dp, peer(k)), device_id_type=MESH)

    def m_arrived(c, k):
        origin = lax.rem(me - k + n, n)
        return pltpu.make_async_remote_copy(
            src_ref=mix_out.at[c, pl.ds(origin * lf, lf)],
            dst_ref=mix_in.at[c, origin],
            send_sem=m_send.at[c, k], recv_sem=m_recv.at[c, k],
            device_id=(dp, origin), device_id_type=MESH)

    def m_own(c):
        return pltpu.make_async_copy(
            mix_out.at[c, pl.ds(me * lf, lf)], mix_in.at[c, me], m_recv.at[c, 0])

    def w_own(which):
        source, stage = shards[which]
        return pltpu.make_async_copy(source, stage.at[dp], loc.at[which])

    for j in range(1, half):
        w_copy(0, j).start()
    for c in range(chunks):
        for k in range(1, n):
            t_copy(c, k).start()
    w_copy(0, 0).start()
    for j in range(half):
        w_copy(1, j).start()
    w_own(0).start()
    w_own(1).start()
    for c in range(chunks):
        t_own(c).start()
    residual = pltpu.make_async_copy(tokens.at[0], tok, loc.at[2])
    residual.start()

    def gather(which, whole):
        stage = shards[which][1]
        for j in range(1, half):
            w_arrived(which, j).wait_recv()
            forward(which, j).start()
        w_own(which).wait()
        w_arrived(which, 0).wait_recv()
        for j in range(1, half):
            forwarded(which, j).wait_recv()
        part = stage.shape[2]
        step = 128

        def place(i, carry):
            rows = pl.ds(pl.multiple_of(i * step, step), step)
            whole[rows, :] = jnp.concatenate([stage[s, rows, :] for s in range(ndp)], axis=1)
            return carry

        lax.fori_loop(0, stage.shape[1] // step, place, 0)

    gather(0, wq)

    block = q_s.shape[1]

    def compute(c, carry):
        t_own(c).wait()
        for k in range(1, n):
            t_arrived(c, k).wait_recv()
        values = recv[c].astype(F32).reshape(frames * ch, width)
        center = jnp.mean(values, axis=-1, keepdims=True)
        moved = values - center
        spread = jnp.mean(jnp.square(moved), axis=-1, keepdims=True)
        normed = (moved * lax.rsqrt(spread + norm_eps) * gain[...]).astype(BF16)

        def split(columns, dest, scale):
            got = jnp.dot(normed, wq[:, columns * HD:(columns + 1) * HD], preferred_element_type=F32)
            if scale is not None:
                got = got * scale
            got = got.reshape(frames, groups, SUB, HD)
            for g in range(groups):
                piece = got[:, g].reshape(frames * SUB, HD).astype(BF16)
                dest[g * (dest.shape[0] // groups):(g + 1) * (dest.shape[0] // groups)] = piece.reshape(
                    dest.shape[0] // groups, dest.shape[1], HD)

        split(0, q_s, 1.0 / math.sqrt(HS))
        split(1, k_s, None)
        split(2, v_s, None)

        def attend(it, inner):
            g = it // nb
            b = lax.rem(it, nb)
            tiles = [None] * (HD // LANES)
            for h in range(HEADS):
                first, last = h * HS, (h + 1) * HS
                lo = first // LANES
                hi = -(-last // LANES)
                cols = slice(lo * LANES, hi * LANES)
                lane = lax.broadcasted_iota(jnp.int32, (block, (hi - lo) * LANES), 1) + lo * LANES
                own = (lane >= first) & (lane < last)
                qh = q_s[it, :, cols].astype(F32)
                qh = jnp.where(own, qh, 0.0).astype(BF16)
                scores = lax.dot_general(
                    qh, k_s[g, :, cols], (((1,), (1,)), ((), ())), preferred_element_type=F32)
                raised = jnp.exp(scores + bias[b])
                probs = (raised / jnp.sum(raised, axis=-1, keepdims=True)).astype(BF16)
                mixed = jnp.dot(probs, v_s[g, :, cols], preferred_element_type=F32)
                for t in range(lo, hi):
                    piece = mixed[:, (t - lo) * LANES:(t - lo + 1) * LANES]
                    if tiles[t] is None:
                        tiles[t] = piece
                    else:
                        inside = own[:, (t - lo) * LANES:(t - lo + 1) * LANES]
                        tiles[t] = jnp.where(inside, piece, tiles[t])
            for t in range(HD // LANES):
                o_s[it, :, t * LANES:(t + 1) * LANES] = tiles[t]
            return inner

        lax.fori_loop(0, groups * nb, attend, 0)
        whole = [o_s[g * nb:(g + 1) * nb].reshape(frames, SUB, HD) for g in range(groups)]
        mix_out[c] = (jnp.concatenate(whole, axis=1) if groups > 1 else whole[0]).astype(BF16)
        for k in range(1, n):
            m_copy(c, k).start()
        m_own(c).start()
        return carry

    lax.fori_loop(0, chunks, compute, 0)
    gather(1, wo)
    residual.wait()

    def finish(c, carry):
        m_own(c).wait()
        for k in range(1, n):
            m_arrived(c, k).wait_recv()
        rows_in = mix_in[c].reshape(n * lf * ch, HD)
        update = jnp.dot(rows_in, wo[...], preferred_element_type=F32).reshape(n, lf, ch, width)
        for s in range(n):
            rows = rows_of(s, c)
            out[0, :, rows, :] = (tok[:, rows, :].astype(F32) + update[s]).astype(BF16)
        return carry

    lax.fori_loop(0, chunks, finish, 0)

    for which in range(2):
        for j in range(half):
            w_copy(which, j).wait_send()
            if j:
                forward(which, j).wait_send()
    for c in range(chunks):
        for k in range(1, n):
            t_copy(c, k).wait_send()
            m_copy(c, k).wait_send()


def shards(n, ndp, tokens, clip_ids, ln_gain, w_qkv, w_out):
    lf, patches, width = tokens.shape[1:]
    frames = n * lf
    lp = patches // n
    ch = 2 * SUB if lp % (2 * SUB) == 0 else SUB
    chunks = lp // ch
    groups = ch // SUB
    rows = frames * SUB
    nb = max(1, rows // 192)
    while rows % nb or (rows // nb) % (2 * SUB):
        nb -= 1
    block = rows // nb
    clip = clip_ids[0]
    lowest = float(jnp.finfo(F32).min)
    place = clip[:, None] * SUB + jnp.arange(SUB, dtype=jnp.int32)[None, :]
    place = place.reshape(rows)
    bias = jnp.where(place[:, None] == place[None, :], 0.0, lowest).astype(F32).reshape(nb, block, rows)
    qcols, ocols = w_qkv.shape[1], w_out.shape[1]
    half = ndp // 2
    vm, dma = pltpu.VMEM, pltpu.SemaphoreType.DMA
    whole = pl.BlockSpec(memory_space=pltpu.VMEM)
    away = pl.BlockSpec(memory_space=pl.ANY)
    return pl.pallas_call(
        functools.partial(kernel, n, ndp, chunks, ch, nb),
        out_shape=jax.ShapeDtypeStruct(tokens.shape, BF16),
        in_specs=[away, away, away, whole, whole],
        out_specs=whole,
        scratch_shapes=[
            vm((chunks, frames, ch, width), BF16),
            vm((chunks, frames, ch, HD), BF16),
            vm((chunks, n, lf, ch, HD), BF16),
            vm((ndp, width, qcols), BF16),
            vm((width, 3 * HD), BF16),
            vm((ndp, HD, ocols), BF16),
            vm((HD, width), BF16),
            vm((groups * nb, block, HD), BF16),
            vm((groups, rows, HD), BF16),
            vm((groups, rows, HD), BF16),
            vm((groups * nb, block, HD), F32),
            vm((lf, patches, width), BF16),
            dma((chunks, n)), dma((chunks, n)), dma((chunks, n)), dma((chunks, n)),
            dma((2, half)), dma((2, half)), dma((2, half)), dma((2, half)), dma((3,)),
        ],
        compiler_params=pltpu.CompilerParams(
            collective_id=0, has_side_effects=True, vmem_limit_bytes=60 * 1024 * 1024),
    )(tokens, w_qkv, w_out, ln_gain.astype(F32).reshape(1, width), bias)


def solution(mesh):
    placed = (P("dp", "seq", None, None), P("dp", None), P(), P(None, "dp"), P(None, "dp"))
    return jax.shard_map(
        functools.partial(shards, mesh.shape["seq"], mesh.shape["dp"]),
        mesh=mesh, in_specs=placed, out_specs=P("dp", "seq", None, None), check_vma=False)
```

time: 152 us -> 82.7 us (0.54)
  Pallas kernels: 0 us -> 72.2 us
  waiting for transfers between devices: 60.1 us -> 0 us
  blocking collectives: 28.2 us -> 0 us
  matrix products: 22 us -> 0 us
  between operations: 13.6 us -> 0.01 us
  starting transfers between devices: 7.45 us -> 0 us
  local copies, waits for them, and re-layouts: 14.9 us -> 8.74 us
  other arithmetic: 5.69 us -> 1.51 us
    pallas_call x0 -> x1, Pallas kernels: none -> 72.2 us  [shards(): pl.pallas_call(functools.partial(kernel, n, ndp, chunks, ch, nb), out_sha...]
    all_to_all x1 -> x0, waiting for transfers between devices: 58.6 us -> none  [shards(): lax.all_to_all(tokens, 'seq', split_axis=2, concat_axis=1, tiled=True)]
    all_to_all x1 -> x0, blocking collectives: 28.2 us -> none  [shards(): lax.all_to_all(mixed.reshape(1, frames, places, HD), 'seq', split_axis=1,...]
    dot_general x4 -> x0, matrix products: 22 us -> none  [the longest x1 8.52 us: column_block(): return jnp.dot(normed, piece, preferred_element_type=jnp.float32)]
    all_to_all x1 -> x0, starting transfers between devices: 7.41 us -> none  [shards(): lax.all_to_all(tokens, 'seq', split_axis=2, concat_axis=1, tiled=True)]
    reshape x4 -> x1, local copies, waits for them, and re-layouts: 6.93 us -> 1.29 us  [shards(): ln_gain.astype(F32).reshape(1, width)]
    convert_element_type x3 -> x0, other arithmetic: 4.62 us -> none  [the longest x1 2.34 us: layer_norm(): values = block.astype(jnp.float32)]
    convert_element_type x2 -> x0, local copies, waits for them, and re-layouts: 2.75 us -> none  [the longest x1 2.42 us: layer_norm(): values = block.astype(jnp.float32)]
  transfers between devices with their start and end apart: 3 -> 0, of which waited for: 1 -> 0; matrix products, arithmetic and copies ran while one was open for 25% -> 0% of each run, Pallas kernels for 0% -> 0%
where the time goes in v1:
time: 82.7 us; the launch traced here: 82.4 us
  Pallas kernels  72.2 us (87%)
  local copies, waits for them, and re-layouts  8.74 us (11%)
  other arithmetic  1.51 us (2%)
    pallas_call x1, Pallas kernels, shards(): pl.pallas_call(functools.partial(kernel, n, ndp, chunks, ch, nb), out_sha...  72.2 us
    unnamed x3, local copies, waits for them, and re-layouts  7.37 us

profile of v1, /device:TPU:0, one launch (start us, length us, event | category | flops | bytes accessed | tf_op | source)
XLA Modules:
  0.0 82.4 jit_solution(16580506288310218898)
XLA Ops:
  0.0 0.7 multiply_bitcast_fusion
  0.7 1.3 %reshape.86.gain = f32[1,1280]{1,0:T(1,128)} reshape(f32[1280]{0:T(1024)} %param.7) | data formatting | bytes 10240 | tf_op jit(solution)/shard_map/reshape | solution.py:299
  1.9 0.1 iota_add_fusion
  2.0 0.1 add.27
  2.1 0.8 compare_select_fusion.bias
  2.9 2.0 %copy.9.w_out = bf16[640,320]{1,0:T(8,128)(2,1)} copy(bf16[640,320]{0,1:T(8,128)(2,1)} %param.9) | data formatting | bytes 819200 | tf_op args[4]
  4.9 2.4 %copy.8.w_qkv = bf16[1280,480]{1,0:T(8,128)(2,1)} copy(bf16[1280,480]{0,1:T(8,128)(2,1)} %param.8) | data formatting | bytes 2457600 | tf_op args[3]
  7.3 72.2 %shard_map.55 = bf16[1,3,256,1280]{3,2,1,0:T(8,128)(2,1)} custom-call(bf16[1,3,256,1280]{3,2,1,0:T(8,128)(2,1)} %tokens.1, bf16[1280,480]{1,0:T(8,128)(2,1)} %copy.8.w_qkv, bf16[640,320]{1,0:T(8,128)(2,1)} %copy.9.w_out, f32[1,1280]{1,0:T(1,128)} %reshape.86.gain, f32[1,192,192]{2,1,0:T(8,128)} %compare_select_fusion.bias), custom_call_target="tpu_custom_call" | custom-call | tf_op jit(solution)/shard_map/pallas_call | solution.py:276
  79.5 2.9 %copy.11 = bf16[1,3,256,1280]{3,2,1,0:T(8,128)(2,1)} copy(bf16[1,3,256,1280]{3,2,1,0:T(8,128)(2,1)} %shard_map.55) | data formatting | bytes 3932160

commit v2 on v1

--- a/solution.py
+++ b/solution.py
@@ -19,8 +19,8 @@
 F32, BF16 = jnp.float32, jnp.bfloat16
 
 
-def kernel(n, ndp, chunks, ch, nb, tokens, w_qkv, w_out, gain, bias, out,
-           recv, mix_out, mix_in, wq_st, wq, wo_st, wo, q_s, k_s, v_s, o_s, tok,
+def kernel(n, ndp, chunks, ch, nb, tokens, w_qkv, w_out, gain, clip, out,
+           recv, mix_out, mix_in, wq_st, wq, wo_st, wo, q_s, k_s, v_s, o_s, bias, tok,
            t_send, t_recv, m_send, m_recv, w_send, w_recv, f_send, f_recv, loc):
     me = lax.axis_index("seq")
     dp = lax.axis_index("dp")
@@ -32,52 +32,61 @@
     groups = ch // SUB
 
     def peer(k):
-        return lax.rem(me + k, n)
+        if n & (n - 1):
+            return lax.rem(me + k, n)
+        other = me
+        bit = 1
+        while bit < n:
+            if k & bit:
+                other = other + bit - 2 * bit * lax.rem(me // bit, 2)
+            bit *= 2
+        return other
+
+    def source_of(k):
+        return lax.rem(me - k + n, n) if n & (n - 1) else peer(k)
+
+    order = range(n - 1, 0, -1)
 
     def far(j):
         return lax.rem(dp + 2 * j, ndp)
 
     barrier = pltpu.get_barrier_semaphore()
-    for k in range(1, n):
+    for k in order:
         pl.semaphore_signal(barrier, inc=1, device_id=(dp, peer(k)), device_id_type=MESH)
     for j in range(1, half):
         pl.semaphore_signal(barrier, inc=1, device_id=(far(j), me), device_id_type=MESH)
     pl.semaphore_signal(barrier, inc=1, device_id=(partner, me), device_id_type=MESH)
     pl.semaphore_wait(barrier, n - 1 + half)
 
-    shards = ((w_qkv, wq_st), (w_out, wo_st))
+    shards = ((w_qkv, wq_st, wq), (w_out, wo_st, wo))
+
+    def slot(which, owner):
+        source, stage, whole = shards[which]
+        part = source.shape[0]
+        if part % (2 * SUB):
+            return stage.at[owner]
+        return whole.at[pl.ds(pl.multiple_of(owner * part, 2 * SUB), part)]
+
+    def w_move(which, j, source, owner, target, send, arrive):
+        return pltpu.make_async_remote_copy(
+            src_ref=source, dst_ref=slot(which, owner),
+            send_sem=send.at[which, j], recv_sem=arrive.at[which, j],
+            device_id=(target, me), device_id_type=MESH)
 
     def w_copy(which, j):
-        source, stage = shards[which]
-        target = far(j) if j else partner
-        return pltpu.make_async_remote_copy(
-            src_ref=source, dst_ref=stage.at[dp],
-            send_sem=w_send.at[which, j], recv_sem=w_recv.at[which, j],
-            device_id=(target, me), device_id_type=MESH)
+        return w_move(which, j, shards[which][0], dp, far(j) if j else partner, w_send, w_recv)
 
     def w_arrived(which, j):
-        source, stage = shards[which]
         origin = lax.rem(dp - 2 * j + ndp, ndp) if j else partner
-        return pltpu.make_async_remote_copy(
-            src_ref=source, dst_ref=stage.at[origin],
-            send_sem=w_send.at[which, j], recv_sem=w_recv.at[which, j],
-            device_id=(partner, me), device_id_type=MESH)
+        return w_move(which, j, shards[which][0], origin, partner, w_send, w_recv)
 
     def forward(which, j):
-        stage = shards[which][1]
         origin = lax.rem(dp - 2 * j + ndp, ndp)
-        return pltpu.make_async_remote_copy(
-            src_ref=stage.at[origin], dst_ref=stage.at[origin],
-            send_sem=f_send.at[which, j], recv_sem=f_recv.at[which, j],
-            device_id=(partner, me), device_id_type=MESH)
+        return w_move(which, j, slot(which, origin), origin, partner, f_send, f_recv)
 
     def forwarded(which, j):
-        stage = shards[which][1]
         origin = lax.rem(partner - 2 * j + ndp, ndp)
-        return pltpu.make_async_remote_copy(
-            src_ref=stage.at[origin], dst_ref=stage.at[origin],
-            send_sem=f_send.at[which, j], recv_sem=f_recv.at[which, j],
-            device_id=(partner, me), device_id_type=MESH)
+        return w_move(which, j, slot(which, origin), origin, partner, f_send, f_recv)
 
     def rows_of(owner, c):
         return pl.ds(pl.multiple_of(owner * lp + c * ch, SUB), ch)
@@ -90,7 +99,7 @@
             device_id=(dp, peer(k)), device_id_type=MESH)
 
     def t_arrived(c, k):
-        origin = lax.rem(me - k + n, n)
+        origin = source_of(k)
         return pltpu.make_async_remote_copy(
             src_ref=tokens.at[0, :, rows_of(origin, c), :],
             dst_ref=recv.at[c, pl.ds(origin * lf, lf)],
@@ -109,7 +118,7 @@
             device_id=(dp, peer(k)), device_id_type=MESH)
 
     def m_arrived(c, k):
-        origin = lax.rem(me - k + n, n)
+        origin = source_of(k)
         return pltpu.make_async_remote_copy(
             src_ref=mix_out.at[c, pl.ds(origin * lf, lf)],
             dst_ref=mix_in.at[c, origin],
@@ -121,13 +130,12 @@
             mix_out.at[c, pl.ds(me * lf, lf)], mix_in.at[c, me], m_recv.at[c, 0])
 
     def w_own(which):
-        source, stage = shards[which]
-        return pltpu.make_async_copy(source, stage.at[dp], loc.at[which])
+        return pltpu.make_async_copy(shards[which][0], slot(which, dp), loc.at[which])
 
     for j in range(1, half):
         w_copy(0, j).start()
     for c in range(chunks):
-        for k in range(1, n):
+        for k in order:
             t_copy(c, k).start()
     w_copy(0, 0).start()
     for j in range(half):
@@ -139,8 +147,8 @@
     residual = pltpu.make_async_copy(tokens.at[0], tok, loc.at[2])
     residual.start()
 
-    def gather(which, whole):
-        stage = shards[which][1]
+    def gather(which):
+        source, stage, whole = shards[which]
         for j in range(1, half):
             w_arrived(which, j).wait_recv()
             forward(which, j).start()
@@ -148,32 +156,41 @@
         w_arrived(which, 0).wait_recv()
         for j in range(1, half):
             forwarded(which, j).wait_recv()
-        part = stage.shape[2]
-        step = 128
-
-        def place(i, carry):
-            rows = pl.ds(pl.multiple_of(i * step, step), step)
-            whole[rows, :] = jnp.concatenate([stage[s, rows, :] for s in range(ndp)], axis=1)
-            return carry
-
-        lax.fori_loop(0, stage.shape[1] // step, place, 0)
-
-    gather(0, wq)
+        part = source.shape[0]
+        if part % (2 * SUB):
+            for owner in range(ndp):
+                whole[owner * part:(owner + 1) * part, :] = stage[owner]
+
+    frames_of = lax.broadcasted_iota(jnp.int32, (frames * SUB, 1), 0)
+    along = lax.broadcasted_iota(jnp.int32, (1, frames * SUB), 1)
+
+    def name(f, carry):
+        down, across = carry
+        return (jnp.where(frames_of // SUB == f, clip[0, f], down),
+                jnp.where(along // SUB == f, clip[0, f], across))
+
+    down, across = lax.fori_loop(
+        0, frames, name, (jnp.zeros_like(frames_of), jnp.zeros_like(along)))
+    same = (down * SUB + frames_of % SUB) == (across * SUB + along % SUB)
+    bias[...] = jnp.where(same, 0.0, float(jnp.finfo(F32).min)).reshape(bias.shape)
+
+    gather(0)
 
     block = q_s.shape[1]
 
     def compute(c, carry):
         t_own(c).wait()
-        for k in range(1, n):
+        for k in order:
             t_arrived(c, k).wait_recv()
         values = recv[c].astype(F32).reshape(frames * ch, width)
         center = jnp.mean(values, axis=-1, keepdims=True)
         moved = values - center
         spread = jnp.mean(jnp.square(moved), axis=-1, keepdims=True)
-        normed = (moved * lax.rsqrt(spread + norm_eps) * gain[...]).astype(BF16)
+        normed = (moved * lax.rsqrt(spread + norm_eps) * gain[...].reshape(1, width)).astype(BF16)
 
         def split(columns, dest, scale):
-            got = jnp.dot(normed, wq[:, columns * HD:(columns + 1) * HD], preferred_element_type=F32)
+            got = lax.dot_general(
+                normed, wq[columns * HD:(columns + 1) * HD, :], (((1,), (1,)), ((), ())), preferred_element_type=F32)
             if scale is not None:
                 got = got * scale
             got = got.reshape(frames, groups, SUB, HD)
@@ -218,21 +235,22 @@
         lax.fori_loop(0, groups * nb, attend, 0)
         whole = [o_s[g * nb:(g + 1) * nb].reshape(frames, SUB, HD) for g in range(groups)]
         mix_out[c] = (jnp.concatenate(whole, axis=1) if groups > 1 else whole[0]).astype(BF16)
-        for k in range(1, n):
+        for k in order:
             m_copy(c, k).start()
         m_own(c).start()
         return carry
 
     lax.fori_loop(0, chunks, compute, 0)
-    gather(1, wo)
+    gather(1)
     residual.wait()
 
     def finish(c, carry):
         m_own(c).wait()
-        for k in range(1, n):
+        for k in order:
             m_arrived(c, k).wait_recv()
         rows_in = mix_in[c].reshape(n * lf * ch, HD)
-        update = jnp.dot(rows_in, wo[...], preferred_element_type=F32).reshape(n, lf, ch, width)
+        update = lax.dot_general(
+            rows_in, wo[...], (((1,), (1,)), ((), ())), preferred_element_type=F32).reshape(n, lf, ch, width)
         for s in range(n):
             rows = rows_of(s, c)
             out[0, :, rows, :] = (tok[:, rows, :].astype(F32) + update[s]).astype(BF16)
@@ -246,7 +264,7 @@
             if j:
                 forward(which, j).wait_send()
     for c in range(chunks):
-        for k in range(1, n):
+        for k in order:
             t_copy(c, k).wait_send()
             m_copy(c, k).wait_send()
 
@@ -263,40 +281,40 @@
     while rows % nb or (rows // nb) % (2 * SUB):
         nb -= 1
     block = rows // nb
-    clip = clip_ids[0]
-    lowest = float(jnp.finfo(F32).min)
-    place = clip[:, None] * SUB + jnp.arange(SUB, dtype=jnp.int32)[None, :]
-    place = place.reshape(rows)
-    bias = jnp.where(place[:, None] == place[None, :], 0.0, lowest).astype(F32).reshape(nb, block, rows)
     qcols, ocols = w_qkv.shape[1], w_out.shape[1]
     half = ndp // 2
     vm, dma = pltpu.VMEM, pltpu.SemaphoreType.DMA
+
+    def staged(columns, depth):
+        return vm((ndp, columns, depth) if columns % (2 * SUB) else (1, 2 * SUB, LANES), BF16)
+
     whole = pl.BlockSpec(memory_space=pltpu.VMEM)
     away = pl.BlockSpec(memory_space=pl.ANY)
     return pl.pallas_call(
         functools.partial(kernel, n, ndp, chunks, ch, nb),
         out_shape=jax.ShapeDtypeStruct(tokens.shape, BF16),
-        in_specs=[away, away, away, whole, whole],
+        in_specs=[away, away, away, whole, pl.BlockSpec(memory_space=pltpu.SMEM)],
         out_specs=whole,
         scratch_shapes=[
             vm((chunks, frames, ch, width), BF16),
             vm((chunks, frames, ch, HD), BF16),
             vm((chunks, n, lf, ch, HD), BF16),
-            vm((ndp, width, qcols), BF16),
-            vm((width, 3 * HD), BF16),
-            vm((ndp, HD, ocols), BF16),
-            vm((HD, width), BF16),
+            staged(qcols, width),
+            vm((3 * HD, width), BF16),
+            staged(ocols, HD),
+            vm((width, HD), BF16),
             vm((groups * nb, block, HD), BF16),
             vm((groups, rows, HD), BF16),
             vm((groups, rows, HD), BF16),
             vm((groups * nb, block, HD), F32),
+            vm((nb, block, rows), F32),
             vm((lf, patches, width), BF16),
             dma((chunks, n)), dma((chunks, n)), dma((chunks, n)), dma((chunks, n)),
             dma((2, half)), dma((2, half)), dma((2, half)), dma((2, half)), dma((3,)),
         ],
         compiler_params=pltpu.CompilerParams(
             collective_id=0, has_side_effects=True, vmem_limit_bytes=60 * 1024 * 1024),
-    )(tokens, w_qkv, w_out, ln_gain.astype(F32).reshape(1, width), bias)
+    )(tokens, w_qkv.T, w_out.T, ln_gain, clip_ids)
 
 
 def solution(mesh):

time: 82.7 us -> 77.7 us (0.940)
  local copies, waits for them, and re-layouts: 8.74 us -> 2.94 us
  Pallas kernels: 72.2 us -> 74.5 us
  other arithmetic: 1.51 us -> 0 us
    unnamed x3 -> x1, local copies, waits for them, and re-layouts: 7.37 us -> 2.94 us
    pallas_call x1, Pallas kernels: 72.2 us -> 74.5 us  [shards(): pl.pallas_call(functools.partial(kernel, n, ndp, chunks, ch, nb), out_sha...]
    reshape x1 -> x0, local copies, waits for them, and re-layouts: 1.29 us -> none  [shards(): ln_gain.astype(F32).reshape(1, width)]
where the time goes in v2:
time: 77.7 us; the launch traced here: 77.5 us
  Pallas kernels  74.5 us (96%)
  local copies, waits for them, and re-layouts  2.94 us (4%)
    pallas_call x1, Pallas kernels, shards(): pl.pallas_call(functools.partial(kernel, n, ndp, chunks, ch, nb), out_sha...  74.5 us
    unnamed x1, local copies, waits for them, and re-layouts  2.94 us

profile of v2, /device:TPU:0, one launch (start us, length us, event | category | flops | bytes accessed | tf_op | source)
XLA Modules:
  0.0 77.5 jit_solution(8212892568586433726)
XLA Ops:
  0.0 74.5 %shard_map.55 = bf16[1,3,256,1280]{3,2,1,0:T(8,128)(2,1)} custom-call(bf16[1,3,256,1280]{3,2,1,0:T(8,128)(2,1)} %tokens.1, bf16[480,1280]{1,0:T(8,128)(2,1)} %bitcast.2, bf16[320,640]{1,0:T(8,128)(2,1)} %bitcast.3, f32[1280]{0:T(1024)} %gain.1, s32[1,24]{1,0:T(1,128)} %clip.1), custom_call_target="tpu_custom_call" | custom-call | tf_op jit(solution)/shard_map/pallas_call | solution.py:293
  74.5 2.9 %copy.7 = bf16[1,3,256,1280]{3,2,1,0:T(8,128)(2,1)} copy(bf16[1,3,256,1280]{3,2,1,0:T(8,128)(2,1)} %shard_map.55) | data formatting | bytes 3932160

commit v3 on v2

--- a/solution.py
+++ b/solution.py
@@ -292,7 +292,7 @@
     away = pl.BlockSpec(memory_space=pl.ANY)
     return pl.pallas_call(
         functools.partial(kernel, n, ndp, chunks, ch, nb),
-        out_shape=jax.ShapeDtypeStruct(tokens.shape, BF16),
+        out_shape=pltpu.VMEM(tokens.shape, BF16),
         in_specs=[away, away, away, whole, pl.BlockSpec(memory_space=pltpu.SMEM)],
         out_specs=whole,
         scratch_shapes=[

time: 77.7 us -> 74.7 us (0.961)
  local copies, waits for them, and re-layouts: 2.94 us -> 1.27 us
  Pallas kernels: 74.5 us -> 73.2 us
    unnamed x1, local copies, waits for them, and re-layouts: 2.94 us -> 1.27 us
    pallas_call x1, Pallas kernels: 74.5 us -> 73.2 us  [shards(): pl.pallas_call(functools.partial(kernel, n, ndp, chunks, ch, nb), out_sha...]
where the time goes in v3:
time: 74.7 us; the launch traced here: 74.5 us
  Pallas kernels  73.2 us (98%)
  local copies, waits for them, and re-layouts  1.27 us (2%)
    pallas_call x1, Pallas kernels, shards(): pl.pallas_call(functools.partial(kernel, n, ndp, chunks, ch, nb), out_sha...  73.2 us

profile of v3, /device:TPU:0, one launch (start us, length us, event | category | flops | bytes accessed | tf_op | source)
XLA Modules:
  0.0 74.5 jit_solution(921811441468349122)
XLA Ops:
  0.0 73.2 %shard_map.55 = bf16[1,3,256,1280]{3,2,1,0:T(8,128)(2,1)S(1)} custom-call(bf16[1,3,256,1280]{3,2,1,0:T(8,128)(2,1)} %tokens.1, bf16[480,1280]{1,0:T(8,128)(2,1)} %bitcast.2, bf16[320,640]{1,0:T(8,128)(2,1)} %bitcast.3, f32[1280]{0:T(1024)} %gain.1, s32[1,24]{1,0:T(1,128)} %clip.1), custom_call_target="tpu_custom_call" | custom-call | tf_op jit(solution)/shard_map/pallas_call | solution.py:293
  73.2 1.3 %copy.7 = bf16[1,3,256,1280]{3,2,1,0:T(8,128)(2,1)} copy(bf16[1,3,256,1280]{3,2,1,0:T(8,128)(2,1)S(1)} %shard_map.55) | data formatting | bytes 3932160
